TPU v7x, 512 devices: a whole 4x8x8 slice. The times are simulated.
512 devices in a mesh: layer: 4 (over x), feat: 32 (over z, y_lo), width: 4 (over y_hi, core).
Axes of the slice: x: 4, y: 8 (y_hi: 2, y_lo: 4; y = y_hi * 4 + y_lo), z: 8, core: 2. Of those that a mesh axis runs over, the one named last changes fastest.
Arguments:
- residuals: bfloat16 [4, 1024, 2304], P('layer', 'feat', 'width'), may hold values from -6 to 6
- cotangent: bfloat16 [4, 1024, 2304], P('layer', 'feat', 'width'), may hold values from -6 to 6
- enc_weight: bfloat16 [4, 2304, 8192], P('layer', 'width', 'feat'), may hold values from -0.125 to 0.125
- enc_bias: float32 [4, 8192], P('layer', 'feat'), may hold values from -3 to 3
- dec_weight: bfloat16 [4, 4, 8192, 2304], P('layer', None, 'feat', 'width'), may hold values from -0.0625 to 0.0625
- active: int32 [4, 1024, 8192], P('layer', None, 'feat'), may hold values 0 or 1
Outputs:
- dec_grad: bfloat16 [4, 4, 8192, 2304], P('layer', None, 'feat', 'width')
- enc_grad: bfloat16 [4, 2304, 8192], P('layer', 'width', 'feat')
- bias_grad: float32 [4, 8192], P('layer', 'feat')
- feat_grad: bfloat16 [4, 1024, 8192], P('layer', None, 'feat')
All inputs are finite; a program needn't handle non-finite values. No bound on the sum of `active` on one device may be relied on, other than what follows from the above.
Results may differ from a plain program's by a relative error of at most 0.005.
Values may be sent and summed in bfloat16 or wider, within the bound.
A program may use at most 64 MiB of HBM per device.

v0:
```python
import jax
import jax.numpy as jnp
from jax import lax
from jax.sharding import PartitionSpec as P


def local(residuals, cotangent, enc_weight, enc_bias, dec_weight, active):
    layers = dec_weight.shape[1]
    source = lax.axis_index("layer")
    local_grads = lax.all_gather(cotangent, "layer", axis=0, tiled=True)
    whole_resid, whole_grads = (
        lax.all_gather(residuals[0], "feat", axis=0, tiled=True),
        lax.all_gather(local_grads, "feat", axis=1, tiled=True),
    )
    later_mask = (jnp.arange(layers) >= source)[:, None, None]
    used_grads = jnp.where(later_mask, whole_grads, jnp.zeros_like(whole_grads))
    enc_part = jnp.dot(whole_resid, enc_weight[0], preferred_element_type=jnp.float32)
    feat_part = jnp.einsum(
        "ktd,kfd->tf", used_grads, dec_weight[0], preferred_element_type=jnp.float32
    )
    enc_total, feat_total = lax.psum((enc_part, feat_part), "width")
    gate_all = active[0].astype(jnp.float32)
    activation = ((enc_total + enc_bias) * gate_all).astype(jnp.bfloat16)
    feat_grad = (feat_total * gate_all).astype(jnp.bfloat16)
    dec_grad = jnp.einsum(
        "tf,ktd->kfd", activation, used_grads, preferred_element_type=jnp.float32
    ).astype(jnp.bfloat16)
    enc_grad = lax.dot_general(
        whole_resid, feat_grad, (((0,), (0,)), ((), ())), preferred_element_type=jnp.float32
    ).astype(jnp.bfloat16)
    bias_grad = jnp.sum(feat_grad, axis=0, dtype=jnp.float32)
    return (dec_grad[None], enc_grad[None], bias_grad[None], feat_grad[None])


def solution(mesh):
    in_specs = (
        P("layer", "feat", "width"),
        P("layer", "feat", "width"),
        P("layer", "width", "feat"),
        P("layer", "feat"),
        P("layer", None, "feat", "width"),
        P("layer", None, "feat"),
    )
    out_specs = (
        P("layer", None, "feat", "width"),
        P("layer", "width", "feat"),
        P("layer", "feat"),
        P("layer", None, "feat"),
    )
    return jax.shard_map(local, mesh=mesh, in_specs=in_specs, out_specs=out_specs, check_vma=False)
```

profile of v0, /device:TPU:1, one launch (start us, length us, event | category | flops | bytes accessed | tf_op | source)
XLA Modules:
  0.0 466.8 jit_solution(9379940428828128747)
XLA Ops:
  7.2 0.0 copy-start
  7.2 0.0 all-gather.6.cloned.1.call-start
  7.2 0.7 all-gather.6.cloned.1.call-update
  7.9 0.0 all-gather.4.cloned.1.call-start
  8.0 12.6 %all_gather.9 = bf16[4,32,576]{2,1,0:T(8,128)(2,1)} all-gather(bf16[1,32,576]{2,1,0:T(8,128)(2,1)} %param.7), channel_id=1, replica_groups=mesh['layer'=4,'feat'=32,'width'=4] {'layer'}, dimensions={0}, use_global_device_ids=true | all-gather | bytes 184320 | tf_op jit(solution)/shard_map/all_gather | solution.py:10
  20.5 0.0 all-gather.4.cloned.1.call-update
  20.6 0.0 all-reduce.3.cloned.1.call-start
  20.6 127.4 %all-gather.6.cloned.1.call-done = bf16[1,1024,576]{2,1,0:T(8,128)(2,1)} async-done(((bf16[1,32,576]{2,1,0:T(8,128)(2,1)}), bf16[1,1024,576]{2,1,0:T(8,128)(2,1)}) %all-gather.6.cloned.1.call-update) | async-done | bytes 1179664 | tf_op jit(solution)/shard_map/all_gather | solution.py:12
  148.0 2.9 fusion.7
  150.9 171.4 %all-gather.4.cloned.1.call-done = bf16[4,1024,576]{2,1,0:T(8,128)(2,1)} async-done(((bf16[4,32,576]{2,1,0:T(8,128)(2,1)}), bf16[4,1024,576]{2,1,0:T(8,128)(2,1)}) %all-gather.4.cloned.1.call-update) | async-done | bytes 4718608 | tf_op jit(solution)/shard_map/all_gather | solution.py:13
  322.3 0.0 copy-done
  322.3 5.2 %fusion.4 = f32[1024,256]{1,0:T(8,128)} fusion(bf16[4,1024,576]{2,1,0:T(8,128)(2,1)} %all-gather.4.cloned.1.call-done, pred[4]{0:T(512)(128)(4,1)S(1)} %iota_compare_fusion, bf16[1,4,256,576]{2,3,1,0:T(8,128)(2,1)S(1)} %copy-done), kind=kOutput, calls=%fused_computation.5 | convolution fusion | flops 1210318848 | bytes 6946820 | tf_op jit(solution)/shard_map/ktd,kfd->tf/dot_general | solution.py:18
  327.4 0.0 copy-start.3
  327.4 0.0 copy-start.1
  327.4 0.0 all-reduce.3.cloned.1.call-update
  327.5 124.2 %all-reduce.3.cloned.1.call-done = (f32[1024,256]{1,0:T(8,128)}, f32[1024,256]{1,0:T(8,128)}) async-done(((f32[1024,256]{1,0:T(8,128)}, f32[1024,256]{1,0:T(8,128)}), (f32[1024,256]{1,0:T(8,128)}, f32[1024,256]{1,0:T(8,128)})) %all-reduce.3.cloned.1.call-update) | async-done | bytes 2097168 | tf_op jit(solution)/shard_map/psum | solution.py:21
  451.7 0.0 copy-done.3
  451.7 0.0 copy-start.4
  451.7 0.0 copy-start.5
  451.7 2.1 convert_reduce_fusion
  453.8 0.0 copy-start.2
  453.8 0.0 copy-done.1
  453.8 1.3 fusion.13
  455.1 0.0 copy-done.4
  455.1 0.0 copy-done.5
  455.1 5.2 %fusion.3 = bf16[1,4,256,576]{2,3,1,0:T(8,128)(2,1)} fusion(bf16[4,1024,576]{2,1,0:T(8,128)(2,1)} %all-gather.4.cloned.1.call-done, pred[4]{0:T(512)(128)(4,1)S(1)} %iota_compare_fusion, s32[1,1024,256]{2,1,0:T(8,128)S(1)} %copy-done.3, f32[1024,256]{1,0:T(8,128)S(1)} %copy-done.4, f32[256]{0:T(256)S(1)} %bitcast.45), kind=kOutput, calls=%fused_computation.4 | convolution fusion | flops 1211957248 | bytes 7996420 | tf_op jit(solution)/shard_map/tf,ktd->kfd/dot_general | solution.py:25
  460.3 0.0 copy-done.2
  (1 shorter events, 0.0 us)
Async XLA Ops:
  7.2 315.1 %copy-start = (bf16[1,4,256,576]{2,3,1,0:T(8,128)(2,1)S(1)}, bf16[1,4,256,576]{2,3,1,0:T(8,128)(2,1)}, u32[]{:S(2)}) copy-start(bf16[1,4,256,576]{2,3,1,0:T(8,128)(2,1)} %param.10) | copy-start | bytes 3538948
  7.2 140.8 %all-gather.6.cloned.1.call-start = ((), (), s32[]{:S(2)}) async-start(), calls=%async_computation.1 | async-start | bytes 1351680 | tf_op jit(solution)/shard_map/all_gather | solution.py:12
  7.9 314.4 %all-gather.4.cloned.1.call-start = ((), (), s32[]{:S(2)}) async-start(), calls=%async_computation | async-start | bytes 5406720 | tf_op jit(solution)/shard_map/all_gather | solution.py:13
  20.6 431.1 %all-reduce.3.cloned.1.call-start = ((), (), s32[]{:S(2)}) async-start(), calls=%async_computation.2 | async-start | bytes 4194304 | tf_op jit(solution)/shard_map/psum | solution.py:21
  327.4 124.2 %copy-start.3 = (s32[1,1024,256]{2,1,0:T(8,128)S(1)}, s32[1,1024,256]{2,1,0:T(8,128)}, u32[]{:S(2)}) copy-start(s32[1,1024,256]{2,1,0:T(8,128)} %param.11) | copy-start | bytes 3145732
  327.4 126.3 %copy-start.1 = (bf16[1,1024,576]{2,1,0:T(8,128)(2,1)S(1)}, bf16[1,1024,576]{2,1,0:T(8,128)(2,1)}, u32[]{:S(2)}) copy-start(bf16[1,1024,576]{2,1,0:T(8,128)(2,1)} %all-gather.6.cloned.1.call-done) | copy-start | bytes 3538948
  451.7 3.4 copy-start.4
  451.7 3.4 copy-start.5
  453.8 6.5 %copy-start.2 = (bf16[1024,256]{1,0:T(8,128)(2,1)}, bf16[1024,256]{1,0:T(8,128)(2,1)S(1)}, u32[]{:S(2)}) copy-start(bf16[1024,256]{1,0:T(8,128)(2,1)S(1)} %get-tuple-element.7) | copy-start | bytes 1572868
Sparse Core Ops, SparseCore 0:
  10.1 137.8 all-gather.5
  150.1 172.1 all-gather.3
  327.6 124.0 all-reduce.2
where the time goes:
time: 467 us
  waiting for transfers between devices  424 us (91%)
  matrix products  14.6 us (3%)
  between operations  13.8 us (3%)
  blocking collectives  12.6 us (3%)
    all_gather x1, waiting for transfers between devices, local(): lax.all_gather(local_grads, 'feat', axis=1, tiled=True)  171 us
    all_gather x1, waiting for transfers between devices, local(): lax.all_gather(residuals[0], 'feat', axis=0, tiled=True)  127 us
    psum x1, waiting for transfers between devices, local(): enc_total, feat_total = lax.psum((enc_part, feat_part), 'width')  124 us
    all_gather x1, blocking collectives, local(): local_grads = lax.all_gather(cotangent, 'layer', axis=0, tiled=True)  12.6 us
  transfers between devices with their start and end apart: 3, of which 3 were waited for; matrix products, arithmetic and copies ran while one was open for 1% of the time, Pallas kernels for 0%

commit v1 on v0

--- a/solution.py
+++ b/solution.py
@@ -2,6 +2,13 @@
 import jax.numpy as jnp
 from jax import lax
 from jax.sharding import PartitionSpec as P
+
+
+def exchange_gather(x, axis, dim):
+    devices = lax.axis_size(axis)
+    shards = jnp.stack([x for _ in range(devices)])
+    shards = lax.all_to_all(shards, axis, split_axis=0, concat_axis=0)
+    return jnp.concatenate(shards, axis=dim)
 
 
 def local(residuals, cotangent, enc_weight, enc_bias, dec_weight, active):
@@ -10,7 +17,7 @@
     local_grads = lax.all_gather(cotangent, "layer", axis=0, tiled=True)
     whole_resid, whole_grads = (
         lax.all_gather(residuals[0], "feat", axis=0, tiled=True),
-        lax.all_gather(local_grads, "feat", axis=1, tiled=True),
+        exchange_gather(local_grads, "feat", 1),
     )
     later_mask = (jnp.arange(layers) >= source)[:, None, None]
     used_grads = jnp.where(later_mask, whole_grads, jnp.zeros_like(whole_grads))

time: 467 us -> 375 us (0.80)
  waiting for transfers between devices: 424 us -> 312 us
  starting transfers between devices: 0.12 us -> 13.8 us
  local copies, waits for them, and re-layouts: 0.03 us -> 8.46 us
    all_gather x1 -> x0, waiting for transfers between devices: 171 us -> none  [local(): lax.all_gather(local_grads, 'feat', axis=1, tiled=True)]
    all_gather x1, waiting for transfers between devices: 127 us -> 174 us  [local(): lax.all_gather(residuals[0], 'feat', axis=0, tiled=True)]
    psum x1, waiting for transfers between devices: 124 us -> 138 us  [local(): enc_total, feat_total = lax.psum((enc_part, feat_part), 'width')]
    all_to_all x0 -> x1, starting transfers between devices: none -> 13.8 us  [exchange_gather(): shards = lax.all_to_all(shards, axis, split_axis=0, concat_axis=0)]
  transfers between devices with their start and end apart: 3 -> 3, of which waited for: 3 -> 2; matrix products, arithmetic and copies ran while one was open for 1% -> 1% of each run, Pallas kernels for 0% -> 0%
where the time goes in v1:
time: 375 us; the launch traced here: 374 us
  waiting for transfers between devices  312 us (83%)
  between operations  14.1 us (4%)
  starting transfers between devices  13.8 us (4%)
  matrix products  12 us (3%)
  blocking collectives  10.7 us (3%)
  local copies, waits for them, and re-layouts  8.46 us (2%)
    all_gather x1, waiting for transfers between devices, local(): lax.all_gather(residuals[0], 'feat', axis=0, tiled=True)  174 us
    psum x1, waiting for transfers between devices, local(): enc_total, feat_total = lax.psum((enc_part, feat_part), 'width')  138 us
    all_to_all x1, starting transfers between devices, exchange_gather(): shards = lax.all_to_all(shards, axis, split_axis=0, concat_axis=0)  13.8 us
    all_gather x1, blocking collectives, local(): local_grads = lax.all_gather(cotangent, 'layer', axis=0, tiled=True)  10.7 us
  transfers between devices with their start and end apart: 3, of which 2 were waited for; matrix products, arithmetic and copies ran while one was open for 1% of the time, Pallas kernels for 0%

profile of v1, /device:TPU:1, one launch (start us, length us, event | category | flops | bytes accessed | tf_op | source)
XLA Modules:
  0.0 374.4 jit_solution(15078776934404905618)
XLA Ops:
  7.2 0.0 copy-start
  7.2 10.7 %all_gather.6 = bf16[4,32,576]{2,1,0:T(8,128)(2,1)S(1)} all-gather(bf16[1,32,576]{2,1,0:T(8,128)(2,1)} %param.7), channel_id=1, replica_groups=mesh['layer'=4,'feat'=32,'width'=4] {'layer'}, dimensions={0}, use_global_device_ids=true | all-gather | bytes 184320 | tf_op jit(solution)/shard_map/all_gather | solution.py:17
  17.9 3.1 stack.2
  20.9 0.0 copy-start.5
  20.9 13.8 %all-to-all-start = ((bf16[32,4,32,576]{3,2,1,0:T(8,128)(2,1)}), bf16[32,4,32,576]{3,2,1,0:T(8,128)(2,1)}, u32[]{:S(2)}, u32[]{:S(2)}) async-start(bf16[32,4,32,576]{3,2,1,0:T(8,128)(2,1)} %stack.2), calls=%async_computation | async-start | bytes 10485760 | tf_op jit(solution)/shard_map/all_to_all | solution.py:10
  34.7 0.0 all-gather.3.cloned.1.call-start
  34.7 0.7 all-gather.3.cloned.1.call-update
  35.4 0.0 all-reduce.3.cloned.1.call-start
  35.5 173.7 %all-gather.3.cloned.1.call-done = bf16[1,1024,576]{2,1,0:T(8,128)(2,1)} async-done(((bf16[1,32,576]{2,1,0:T(8,128)(2,1)}), bf16[1,1024,576]{2,1,0:T(8,128)(2,1)}) %all-gather.3.cloned.1.call-update) | async-done | bytes 1179664 | tf_op jit(solution)/shard_map/all_gather | solution.py:19
  209.1 0.0 copy-done.5
  209.1 2.9 fusion.3
  212.0 0.0 all-to-all-done
  212.0 3.1 copy.13
  215.1 0.9 bitcast_select_fusion
  216.0 0.0 copy-start.1
  216.0 2.3 copy-done.1
  218.3 0.0 copy-done
  218.3 2.4 convolution_bitcast_fusion
  220.7 0.0 copy-start.4
  220.7 0.0 copy-start.7
  220.7 0.0 all-reduce.3.cloned.1.call-update
  220.8 138.0 %all-reduce.3.cloned.1.call-done = (f32[1024,256]{1,0:T(8,128)}, f32[1024,256]{1,0:T(8,128)}) async-done(((f32[1024,256]{1,0:T(8,128)}, f32[1024,256]{1,0:T(8,128)}), (f32[1024,256]{1,0:T(8,128)}, f32[1024,256]{1,0:T(8,128)})) %all-reduce.3.cloned.1.call-update) | async-done | bytes 2097168 | tf_op jit(solution)/shard_map/psum | solution.py:28
  358.8 0.0 copy-start.6
  358.8 0.0 copy-done.4
  358.8 2.1 convert_reduce_fusion
  360.9 0.0 copy-start.3
  360.9 0.0 copy-done.7
  360.9 0.0 copy-done.6
  360.9 0.0 copy-start.2
  360.9 5.3 %fusion = bf16[1,4,256,576]{2,3,1,0:T(8,128)(2,1)} fusion(bf16[4,1024,576]{2,1,0:T(8,128)(2,1)} %copy-done.1, s32[1,1024,256]{2,1,0:T(8,128)S(1)} %copy-done.4, f32[1024,256]{1,0:T(8,128)S(1)} %copy-done.6, f32[256]{0:T(256)S(1)} %bitcast.50), kind=kOutput, calls=%fused_computation.2 | convolution fusion | flops 1209597952 | bytes 7996416 | tf_op jit(solution)/shard_map/tf,ktd->kfd/dot_general | solution.py:32
  366.2 0.0 copy-done.3
  366.2 0.0 copy-done.2
  366.2 1.4 fusion.9
  (1 shorter events, 0.0 us)
Async XLA Ops:
  7.2 211.1 %copy-start = (bf16[1,4,256,576]{2,3,1,0:T(8,128)(2,1)S(1)}, bf16[1,4,256,576]{2,3,1,0:T(8,128)(2,1)}, u32[]{:S(2)}) copy-start(bf16[1,4,256,576]{2,3,1,0:T(8,128)(2,1)} %param.10) | copy-start | bytes 3538948
  20.9 188.2 %copy-start.5 = (bf16[1,576,256]{2,1,0:T(8,128)(2,1)S(1)}, bf16[1,576,256]{2,1,0:T(8,128)(2,1)}, u32[]{:S(2)}) copy-start(bf16[1,576,256]{2,1,0:T(8,128)(2,1)} %param.8) | copy-start | bytes 884740
  20.9 191.1 %all-to-all-start = ((bf16[32,4,32,576]{3,2,1,0:T(8,128)(2,1)}), bf16[32,4,32,576]{3,2,1,0:T(8,128)(2,1)}, u32[]{:S(2)}, u32[]{:S(2)}) async-start(bf16[32,4,32,576]{3,2,1,0:T(8,128)(2,1)} %stack.2), calls=%async_computation | async-start | bytes 10485760 | tf_op jit(solution)/shard_map/all_to_all | solution.py:10
  34.7 174.5 %all-gather.3.cloned.1.call-start = ((), (), s32[]{:S(2)}) async-start(), calls=%async_computation.1 | async-start | bytes 1351680 | tf_op jit(solution)/shard_map/all_gather | solution.py:19
  35.4 323.4 %all-reduce.3.cloned.1.call-start = ((), (), s32[]{:S(2)}) async-start(), calls=%async_computation.2 | async-start | bytes 4194304 | tf_op jit(solution)/shard_map/psum | solution.py:28
  216.0 2.3 copy-start.1
  220.7 138.1 %copy-start.4 = (s32[1,1024,256]{2,1,0:T(8,128)S(1)}, s32[1,1024,256]{2,1,0:T(8,128)}, u32[]{:S(2)}) copy-start(s32[1,1024,256]{2,1,0:T(8,128)} %param.11) | copy-start | bytes 3145732
  220.7 140.2 %copy-start.7 = (f32[1,256]{1,0:T(1,128)S(1)}, f32[1,256]{1,0:T(1,128)}, u32[]{:S(2)}) copy-start(f32[1,256]{1,0:T(1,128)} %param.9) | copy-start | bytes 3076
  358.8 2.1 copy-start.6
  360.9 5.4 %copy-start.3 = (bf16[1024,256]{1,0:T(8,128)(2,1)}, bf16[1024,256]{1,0:T(8,128)(2,1)S(1)}, u32[]{:S(2)}) copy-start(bf16[1024,256]{1,0:T(8,128)(2,1)S(1)} %get-tuple-element.7) | copy-start | bytes 1572868
  360.9 5.4 %copy-start.2 = (bf16[1,1024,576]{2,1,0:T(8,128)(2,1)S(1)}, bf16[1,1024,576]{2,1,0:T(8,128)(2,1)}, u32[]{:S(2)}) copy-start(bf16[1,1024,576]{2,1,0:T(8,128)(2,1)} %all-gather.3.cloned.1.call-done) | copy-start | bytes 3538948
Sparse Core Ops, SparseCore 0:
  37.6 171.5 all-gather.2
  220.9 137.8 all-reduce.2
